TPU v7x, 512 devices: a whole 4x8x8 slice. The times are simulated.
512 devices in a mesh: grp: 32 (over y_lo, z, core), blk: 16 (over x, y_hi).
Axes of the slice: x: 4, y: 8 (y_hi: 4, y_lo: 2; y = y_hi * 2 + y_lo), z: 8, core: 2. Of those that a mesh axis runs over, the one named last changes fastest.
Arguments:
- child_inverse: bfloat16 [32, 2, 2048, 2048], P('grp', None, 'blk'), may hold values from -0.09375 to 0.09375
- border_block: bfloat16 [32, 2, 2048, 2048], P('grp', None, 'blk'), may hold values from -0.09375 to 0.09375
- child_rhs: bfloat16 [32, 2, 2048, 256], P('grp', None, 'blk'), may hold values from -6 to 6
- parent_inverse: bfloat16 [32, 2, 4096, 2048], P('grp', None, 'blk'), may hold values from -0.0625 to 0.0625
- parent_rhs: bfloat16 [32, 2, 2048, 256], P('grp', None, 'blk'), may hold values from -6 to 6
- parent_of: int32 [32, 1], replicated, may hold values from 0 to 15
- owner: int32 [16], replicated, may hold values from 0 to 15, each once
- row_map: int32 [32, 2048], replicated, may hold values from 0 to 4095, as said below
Outputs:
- child_solution: bfloat16 [32, 2, 2048, 256], P('grp', None, 'blk')
- parent_solution: bfloat16 [32, 2, 2048, 256], P('grp', None, 'blk')
Inputs may be any that keep to these rules, and one draw needn't show every extreme that they name: parent_of[c, 0] is the parent front of the sibling front on group c; every parent front has one sibling or more. owner[p] names the pair of groups 2 owner[p] and 2 owner[p] + 1 that holds parent front p; each pair holds one parent. row_map[c, j] differ for different j of one c; border row j with j // 128 = b goes to a parent row h * 2048 + b * 128 + r with h of 0 or 1 and r < 128.
All inputs are finite; a program needn't handle non-finite values.
Results may differ from a plain program's by a relative error of at most 0.008.
Values may be sent and summed in bfloat16 or wider, within the bound.
No kernel may reach another device: no remote copies, remote signals or barrier semaphores. Data moves between devices by JAX's collectives and lax.ppermute only.
A program may use at most 64 MiB of HBM per device.

v0:
```python
import jax
import jax.numpy as jnp
from jax import lax
from jax.sharding import PartitionSpec as P


def swapped(shard, axis, stride):
    return lax.ppermute(shard, axis, [(i, i ^ 1 << stride) for i in range(lax.axis_size(axis))])


def complex_product(left, right):
    real_part = jnp.dot(left[0], right[0], preferred_element_type=jnp.float32) - jnp.dot(
        left[1], right[1], preferred_element_type=jnp.float32
    )
    imag_part = jnp.dot(left[0], right[1], preferred_element_type=jnp.float32) + jnp.dot(
        left[1], right[0], preferred_element_type=jnp.float32
    )
    return jnp.stack([real_part, imag_part])


def column_fold(matrix, shard_piece):
    return complex_product(matrix, shard_piece)


def per_device(
    child_inverse, border_block, child_rhs, parent_inverse, parent_rhs, parent_of, owner, row_map
):
    inverse_rows = child_inverse[0]
    border_rows_block = border_block[0]
    child_solved = column_fold(
        inverse_rows, lax.all_gather(child_rhs[0], "blk", axis=1, tiled=True)
    ).astype(jnp.bfloat16)
    update_rows = (
        -column_fold(border_rows_block, lax.all_gather(child_solved, "blk", axis=1, tiled=True))
    ).astype(jnp.bfloat16)
    group_index = lax.axis_index("grp")
    slot_index = lax.axis_index("blk")
    column_half = group_index % 2
    my_pair = group_index // 2
    border_count = update_rows.shape[1]
    half_rows = parent_rhs.shape[2]
    half_order = parent_inverse.shape[3]
    destination = owner[parent_of[:, 0]]
    local_map = lax.dynamic_slice_in_dim(row_map, slot_index * border_count, border_count, 1)
    row_base = slot_index * half_rows
    offsets = jnp.arange(half_rows, dtype=jnp.int32)
    wanted_rows = column_half * half_order + row_base + offsets
    matches = (local_map[:, None, :] == wanted_rows[None, :, None]) & (destination == my_pair)[
        :, None, None
    ]
    onehot_table = matches.astype(jnp.bfloat16)
    received_sums = jnp.einsum(
        "krj,kcjs->crs",
        onehot_table,
        lax.all_gather(update_rows[None], "grp", axis=0, tiled=True),
        preferred_element_type=jnp.float32,
    )
    right_side = (parent_rhs[0].astype(jnp.float32) + received_sums).astype(jnp.bfloat16)
    parent_block = parent_inverse[0]
    partial_value = column_fold(parent_block, lax.all_gather(right_side, "blk", axis=1, tiled=True))
    partner_part = swapped(partial_value.astype(jnp.bfloat16), "grp", 0).astype(partial_value.dtype)
    combined = partial_value + partner_part
    own_rows = lax.dynamic_slice_in_dim(combined, column_half * half_rows, half_rows, 1)
    return (child_solved[None], own_rows.astype(jnp.bfloat16)[None])


def solution(mesh):
    in_specs = (
        P("grp", None, "blk", None),
        P("grp", None, "blk", None),
        P("grp", None, "blk", None),
        P("grp", None, "blk", None),
        P("grp", None, "blk", None),
        P(),
        P(),
        P(),
    )
    out_specs = (P("grp", None, "blk", None), P("grp", None, "blk", None))
    return jax.shard_map(
        per_device, mesh=mesh, in_specs=in_specs, out_specs=out_specs, check_vma=False
    )
```

profile of v0, /device:TPU:1, one launch (start us, length us, event | category | flops | bytes accessed | tf_op | source)
XLA Modules:
  0.0 306.5 jit_solution(10172488542410082918)
XLA Ops:
  7.2 0.7 all-gather.12.cloned.1.call-update
  8.0 72.5 %all-gather.12.cloned.1.call-done = bf16[1,2,2048,256]{3,2,1,0:T(8,128)(2,1)} async-done(((bf16[1,2,128,256]{3,2,1,0:T(8,128)(2,1)}), bf16[1,2,2048,256]{3,2,1,0:T(8,128)(2,1)}) %all-gather.12.cloned.1.call-update) | async-done | bytes 2097168 | tf_op jit(solution)/shard_map/all_gather | solution.py:31
  80.5 1.8 fusion.28
  82.3 1.5 fusion.29
  84.2 0.3 fusion.18
  84.5 0.7 pad_maximum_fusion.2
  85.3 62.4 %all-gather.6.cloned.1.call-done = bf16[2,2048,256]{2,1,0:T(8,128)(2,1)} async-done(((bf16[2,128,256]{2,1,0:T(8,128)(2,1)}), bf16[2,2048,256]{2,1,0:T(8,128)(2,1)}) %all-gather.6.cloned.1.call-update) | async-done | bytes 2097168 | tf_op jit(solution)/shard_map/all_gather | solution.py:34
  147.6 1.8 fusion.30
  149.5 0.5 fusion.31
  150.0 0.5 fusion.16
  150.5 0.5 fusion.15
  151.0 0.8 copy.17
  152.1 0.7 gather_fusion
  152.8 67.6 %all-gather.8.cloned.1.call-done = bf16[32,2,128,256]{3,2,1,0:T(8,128)(2,1)} async-done(((bf16[1,2,128,256]{3,2,1,0:T(8,128)(2,1)}), bf16[32,2,128,256]{3,2,1,0:T(8,128)(2,1)}) %all-gather.8.cloned.1.call-update) | async-done | bytes 4194320 | tf_op jit(solution)/shard_map/all_gather | solution.py:55
  220.4 4.3 %fusion.12 = bf16[2,128,256]{1,2,0:T(8,128)(2,1)} fusion(bf16[32,2,128,256]{3,2,1,0:T(8,128)(2,1)} %all-gather.8.cloned.1.call-done, s32[32,128]{1,0:T(8,128)S(1)} %constant_dynamic-slice_fusion, s32[128]{0:T(128)S(1)} %iota_add_fusion, pred[32]{0:T(512)(128)(4,1)S(1)} %broadcast_compare_fusion, bf16[1,2,128,256]{2,3,1,0:T(8,128)(2,1)S(1)} %copy.16), kind=kOutput, calls=%fused_computation.11 | convolution fusion | flops 538116096 | bytes 4473376 | tf_op jit(solution)/shard_map/krj,kcjs->crs/dot_general | solution.py:52
  224.7 64.1 %all-gather.10.cloned.1.call-done = bf16[2,2048,256]{1,2,0:T(8,128)(2,1)} async-done(((bf16[2,128,256]{1,2,0:T(8,128)(2,1)}), bf16[2,2048,256]{1,2,0:T(8,128)(2,1)}) %all-gather.10.cloned.1.call-update) | async-done | bytes 2097168 | tf_op jit(solution)/shard_map/all_gather | solution.py:60
  288.8 1.8 fusion.23
  290.7 0.5 fusion.21
  291.2 0.5 fusion.8
  291.7 0.5 fusion.7
  292.2 5.8 %collective-permute-start = (bf16[2,256,256]{1,2,0:T(8,128)(2,1)S(1)}, bf16[2,256,256]{1,2,0:T(8,128)(2,1)S(1)}, u32[]{:S(2)}, u32[]{:S(2)}) collective-permute-start(bf16[2,256,256]{1,2,0:T(8,128)(2,1)S(1)} %fusion.36), channel_id=1, source_target_pairs={{0,16},{16,0},{32,48},{48,32},{64,80},{80,64},{96,112},{112,96},{1... | collective-permute-start | bytes 786440 | tf_op jit(solution)/shard_map/ppermute | solution.py:8
  298.0 0.7 pad_maximum_fusion.1
  298.7 0.5 collective-permute-done
  299.2 0.8 copy.19
  (37 shorter events, 0.9 us)
Async XLA Ops:
  7.2 145.6 %copy-start = (s32[32,2048]{1,0:T(8,128)S(1)}, s32[32,2048]{1,0:T(8,128)}, u32[]{:S(2)}) copy-start(s32[32,2048]{1,0:T(8,128)} %param.15) | copy-start | bytes 786436
  7.2 75.1 %copy-start.7 = (bf16[1,2,128,2048]{3,2,1,0:T(8,128)(2,1)S(1)}, bf16[1,2,128,2048]{3,2,1,0:T(8,128)(2,1)}, u32[]{:S(2)}) copy-start(bf16[1,2,128,2048]{3,2,1,0:T(8,128)(2,1)} %param.8) | copy-start | bytes 3145732
  7.2 73.3 %all-gather.12.cloned.1.call-start = ((), (), s32[]{:S(2)}) async-start(), calls=%async_computation.3 | async-start | bytes 2228224 | tf_op jit(solution)/shard_map/all_gather | solution.py:31
  7.9 139.7 %all-gather.6.cloned.1.call-start = ((), (), s32[]{:S(2)}) async-start(), calls=%async_computation | async-start | bytes 2228224 | tf_op jit(solution)/shard_map/all_gather | solution.py:34
  80.5 3.4 %copy-start.5 = (bf16[1,2,2048,256]{3,2,1,0:T(8,128)(2,1)S(1)}, bf16[1,2,2048,256]{3,2,1,0:T(8,128)(2,1)}, u32[]{:S(2)}) copy-start(bf16[1,2,2048,256]{3,2,1,0:T(8,128)(2,1)} %all-gather.12.cloned.1.call-done) | copy-start | bytes 6291460
  83.9 63.8 %copy-start.8 = (bf16[1,2,128,2048]{3,2,1,0:T(8,128)(2,1)S(1)}, bf16[1,2,128,2048]{3,2,1,0:T(8,128)(2,1)}, u32[]{:S(2)}) copy-start(bf16[1,2,128,2048]{3,2,1,0:T(8,128)(2,1)} %param.9) | copy-start | bytes 3145732
  85.2 135.2 %all-gather.8.cloned.1.call-start = ((), (), s32[]{:S(2)}) async-start(), calls=%async_computation.1 | async-start | bytes 4325376 | tf_op jit(solution)/shard_map/all_gather | solution.py:55
  147.6 1.9 copy-start.4
  150.5 1.4 copy-start.2
  150.5 1.6 copy-start.9
  150.5 1.6 copy-start.1
  151.8 137.0 %all-gather.10.cloned.1.call-start = ((), (), s32[]{:S(2)}) async-start(), calls=%async_computation.2 | async-start | bytes 2228224 | tf_op jit(solution)/shard_map/all_gather | solution.py:60
  152.8 136.0 %copy-start.3 = (bf16[1,2,256,2048]{3,2,1,0:T(8,128)(2,1)S(1)}, bf16[1,2,256,2048]{3,2,1,0:T(8,128)(2,1)}, u32[]{:S(2)}) copy-start(bf16[1,2,256,2048]{3,2,1,0:T(8,128)(2,1)} %param.11) | copy-start | bytes 6291460
  288.8 1.9 copy-start.6
  292.2 6.9 %collective-permute-start = (bf16[2,256,256]{1,2,0:T(8,128)(2,1)S(1)}, bf16[2,256,256]{1,2,0:T(8,128)(2,1)S(1)}, u32[]{:S(2)}, u32[]{:S(2)}) collective-permute-start(bf16[2,256,256]{1,2,0:T(8,128)(2,1)S(1)} %fusion.36), channel_id=1, source_target_pairs={{0,16},{16,0},{32,48},{48,32},{64,80},{80,64},{96,112},{112,96},{1... | collective-permute-start | bytes 786440 | tf_op jit(solution)/shard_map/ppermute | solution.py:8
Sparse Core Ops, SparseCore 0:
  11.1 69.3 all-gather.11
  85.3 62.2 all-gather.5
  151.9 68.4 all-gather.7
  224.8 63.9 all-gather.9
where the time goes:
time: 307 us; the launch traced here: 306 us
  waiting for transfers between devices  268 us (87%)
  matrix products  14.8 us (5%)
  between operations  14.1 us (5%)
  starting transfers between devices  5.96 us (2%)
    all_gather x1, waiting for transfers between devices, per_device(): lax.all_gather(child_rhs[0], 'blk', axis=1, tiled=True)  72.5 us
    all_gather x1, waiting for transfers between devices, per_device(): lax.all_gather(update_rows[None], 'grp', axis=0, tiled=True)  67.6 us
    all_gather x1, waiting for transfers between devices, per_device(): lax.all_gather(right_side, 'blk', axis=1, tiled=True)  64.1 us
    all_gather x1, waiting for transfers between devices, per_device(): lax.all_gather(child_solved, 'blk', axis=1, tiled=True)  62.4 us
  transfers between devices with their start and end apart: 5, of which 5 were waited for; matrix products, arithmetic and copies ran while one was open for 0% of the time, Pallas kernels for 0%

commit v1 on v0

--- a/solution.py
+++ b/solution.py
@@ -27,9 +27,14 @@
 ):
     inverse_rows = child_inverse[0]
     border_rows_block = border_block[0]
-    child_solved = column_fold(
-        inverse_rows, lax.all_gather(child_rhs[0], "blk", axis=1, tiled=True)
-    ).astype(jnp.bfloat16)
+
+    def treat_sheets(z_in, dimension_no):
+        everything = tuple((z_in for _ in range(lax.axis_size("blk"))))
+        earlier = jnp.stack(everything, 0)
+        q_next = lax.all_to_all(earlier, "blk", 0, 0)
+        return jnp.concatenate(q_next, dimension_no)
+
+    child_solved = column_fold(inverse_rows, treat_sheets(child_rhs[0], 1)).astype(jnp.bfloat16)
     update_rows = (
         -column_fold(border_rows_block, lax.all_gather(child_solved, "blk", axis=1, tiled=True))
     ).astype(jnp.bfloat16)

time: 307 us -> 296 us (0.964)
  waiting for transfers between devices: 268 us -> 196 us
  blocking collectives: 0 us -> 61 us
    all_gather x1 -> x0, waiting for transfers between devices: 72.5 us -> none  [per_device(): lax.all_gather(child_rhs[0], 'blk', axis=1, tiled=True)]
    all_to_all x0 -> x1, blocking collectives: none -> 61 us  [treat_sheets(): q_next = lax.all_to_all(earlier, 'blk', 0, 0)]
  transfers between devices with their start and end apart: 5 -> 4, of which waited for: 5 -> 4; matrix products, arithmetic and copies ran while one was open for 0% -> 1% of each run, Pallas kernels for 0% -> 0%
where the time goes in v1:
time: 296 us; the launch traced here: 295 us
  waiting for transfers between devices  196 us (66%)
  blocking collectives  61 us (21%)
  between operations  14 us (5%)
  matrix products  12 us (4%)
  starting transfers between devices  5.93 us (2%)
  local copies, waits for them, and re-layouts  4.91 us (2%)
    all_gather x1, waiting for transfers between devices, per_device(): lax.all_gather(update_rows[None], 'grp', axis=0, tiled=True)  67.6 us
    all_gather x1, waiting for transfers between devices, per_device(): lax.all_gather(right_side, 'blk', axis=1, tiled=True)  64.1 us
    all_gather x1, waiting for transfers between devices, per_device(): lax.all_gather(child_solved, 'blk', axis=1, tiled=True)  63.9 us
    all_to_all x1, blocking collectives, treat_sheets(): q_next = lax.all_to_all(earlier, 'blk', 0, 0)  61 us
  transfers between devices with their start and end apart: 4, of which 4 were waited for; matrix products, arithmetic and copies ran while one was open for 1% of the time, Pallas kernels for 0%

profile of v1, /device:TPU:1, one launch (start us, length us, event | category | flops | bytes accessed | tf_op | source)
XLA Modules:
  0.0 295.4 jit_solution(4751731415797952556)
XLA Ops:
  7.2 1.2 stack.39
  8.4 61.0 %all_to_all.5 = bf16[16,2,128,256]{3,2,1,0:T(8,128)(2,1)S(1)} all-to-all(bf16[16,2,128,256]{3,2,1,0:T(8,128)(2,1)S(1)} %stack.39), channel_id=1, replica_groups=mesh['grp'=32,'blk'=16] {'blk'}, dimensions={0} | all-to-all | bytes 4194304 | tf_op jit(solution)/shard_map/all_to_all | solution.py:34
  69.6 1.0 copy-done.2
  71.3 0.3 fusion.17
  71.6 0.3 fusion.18
  71.9 0.7 pad_maximum_fusion.2
  72.7 63.9 %all-gather.4.cloned.1.call-done = bf16[2,2048,256]{2,1,0:T(8,128)(2,1)} async-done(((bf16[2,128,256]{2,1,0:T(8,128)(2,1)}), bf16[2,2048,256]{2,1,0:T(8,128)(2,1)}) %all-gather.4.cloned.1.call-update) | async-done | bytes 2097168 | tf_op jit(solution)/shard_map/all_gather | solution.py:39
  136.6 1.8 fusion.28
  138.5 0.5 fusion.29
  138.9 0.5 fusion.16
  139.5 0.5 fusion.15
  140.0 0.8 copy.17
  141.0 0.7 gather_fusion
  141.8 67.6 %all-gather.6.cloned.1.call-done = bf16[32,2,128,256]{3,2,1,0:T(8,128)(2,1)} async-done(((bf16[1,2,128,256]{3,2,1,0:T(8,128)(2,1)}), bf16[32,2,128,256]{3,2,1,0:T(8,128)(2,1)}) %all-gather.6.cloned.1.call-update) | async-done | bytes 4194320 | tf_op jit(solution)/shard_map/all_gather | solution.py:60
  209.3 4.3 %fusion.12 = bf16[2,128,256]{1,2,0:T(8,128)(2,1)} fusion(bf16[32,2,128,256]{3,2,1,0:T(8,128)(2,1)} %all-gather.6.cloned.1.call-done, s32[32,128]{1,0:T(8,128)S(1)} %constant_dynamic-slice_fusion, s32[128]{0:T(128)S(1)} %iota_add_fusion, pred[32]{0:T(512)(128)(4,1)S(1)} %broadcast_compare_fusion, bf16[1,2,128,256]{2,3,1,0:T(8,128)(2,1)S(1)} %copy.16), kind=kOutput, calls=%fused_computation.11 | convolution fusion | flops 538116096 | bytes 4473376 | tf_op jit(solution)/shard_map/krj,kcjs->crs/dot_general | solution.py:57
  213.6 64.1 %all-gather.8.cloned.1.call-done = bf16[2,2048,256]{1,2,0:T(8,128)(2,1)} async-done(((bf16[2,128,256]{1,2,0:T(8,128)(2,1)}), bf16[2,2048,256]{1,2,0:T(8,128)(2,1)}) %all-gather.8.cloned.1.call-update) | async-done | bytes 2097168 | tf_op jit(solution)/shard_map/all_gather | solution.py:65
  277.7 1.8 fusion.23
  279.7 0.5 fusion.21
  280.1 0.5 fusion.8
  280.6 0.5 fusion.7
  281.1 5.8 %collective-permute-start = (bf16[2,256,256]{1,2,0:T(8,128)(2,1)S(1)}, bf16[2,256,256]{1,2,0:T(8,128)(2,1)S(1)}, u32[]{:S(2)}, u32[]{:S(2)}) collective-permute-start(bf16[2,256,256]{1,2,0:T(8,128)(2,1)S(1)} %fusion.34), channel_id=1, source_target_pairs={{0,16},{16,0},{32,48},{48,32},{64,80},{80,64},{96,112},{112,96},{1... | collective-permute-start | bytes 786440 | tf_op jit(solution)/shard_map/ppermute | solution.py:8
  286.9 0.7 pad_maximum_fusion.1
  287.6 0.5 collective-permute-done
  288.1 0.8 copy.19
  (35 shorter events, 1.4 us)
Async XLA Ops:
  7.2 134.6 %copy-start = (s32[32,2048]{1,0:T(8,128)S(1)}, s32[32,2048]{1,0:T(8,128)}, u32[]{:S(2)}) copy-start(s32[32,2048]{1,0:T(8,128)} %param.15) | copy-start | bytes 786436
  7.2 129.4 %all-gather.4.cloned.1.call-start = ((), (), s32[]{:S(2)}) async-start(), calls=%async_computation.1 | async-start | bytes 2228224 | tf_op jit(solution)/shard_map/all_gather | solution.py:39
  69.4 1.2 copy-start.2
  71.3 65.3 %copy-start.7 = (bf16[1,2,128,2048]{3,2,1,0:T(8,128)(2,1)S(1)}, bf16[1,2,128,2048]{3,2,1,0:T(8,128)(2,1)}, u32[]{:S(2)}) copy-start(bf16[1,2,128,2048]{3,2,1,0:T(8,128)(2,1)} %param.9) | copy-start | bytes 3145732
  72.6 136.7 %all-gather.6.cloned.1.call-start = ((), (), s32[]{:S(2)}) async-start(), calls=%async_computation.2 | async-start | bytes 4325376 | tf_op jit(solution)/shard_map/all_gather | solution.py:60
  136.6 1.9 copy-start.5
  139.4 1.4 copy-start.3
  139.4 1.6 copy-start.8
  139.4 1.6 copy-start.1
  140.8 137.0 %all-gather.8.cloned.1.call-start = ((), (), s32[]{:S(2)}) async-start(), calls=%async_computation.3 | async-start | bytes 2228224 | tf_op jit(solution)/shard_map/all_gather | solution.py:65
  141.8 136.0 %copy-start.4 = (bf16[1,2,256,2048]{3,2,1,0:T(8,128)(2,1)S(1)}, bf16[1,2,256,2048]{3,2,1,0:T(8,128)(2,1)}, u32[]{:S(2)}) copy-start(bf16[1,2,256,2048]{3,2,1,0:T(8,128)(2,1)} %param.11) | copy-start | bytes 6291460
  277.7 1.9 copy-start.6
  281.1 7.0 %collective-permute-start = (bf16[2,256,256]{1,2,0:T(8,128)(2,1)S(1)}, bf16[2,256,256]{1,2,0:T(8,128)(2,1)S(1)}, u32[]{:S(2)}, u32[]{:S(2)}) collective-permute-start(bf16[2,256,256]{1,2,0:T(8,128)(2,1)S(1)} %fusion.34), channel_id=1, source_target_pairs={{0,16},{16,0},{32,48},{48,32},{64,80},{80,64},{96,112},{112,96},{1... | collective-permute-start | bytes 786440 | tf_op jit(solution)/shard_map/ppermute | solution.py:8
Sparse Core Ops, SparseCore 0:
  72.8 63.7 all-gather.3
  140.9 68.4 all-gather.5
  213.8 63.9 all-gather.7
